TPU v7x, 1024 devices: a whole 4x4x32 slice. The times are simulated.
1024 devices in a mesh: dp: 16 (over y, x), ctx: 64 (over z, core).
Axes of the slice: x: 4, y: 4, z: 32, core: 2. Of those that a mesh axis runs over, the one named last changes fastest.
Arguments:
- segment_ids: int32 [16, 8192], P('dp'), may hold values from 0 to 63, never falling along the last dimension, each value on 1 to 512 neighbouring positions
- queries: bfloat16 [16, 8192, 2048], P('dp', 'ctx'), may hold values from -600 to 600
- keys: bfloat16 [16, 8192, 1024], P('dp', 'ctx'), may hold values from -600 to 600
- values: bfloat16 [16, 8192, 1024], P('dp', 'ctx'), may hold values from -6 to 6
- query_gain: float32 [256], replicated, may hold values from 0.1 to 1.9
- key_gain: float32 [256], replicated, may hold values from 0.1 to 1.9
- out_grad: bfloat16 [16, 8192, 2048], P('dp', 'ctx'), may hold values from -9 to 9
Outputs:
- attended: bfloat16 [16, 8192, 2048], P('dp', 'ctx')
- query_grad: bfloat16 [16, 8192, 2048], P('dp', 'ctx')
- key_grad: bfloat16 [16, 8192, 1024], P('dp', 'ctx')
- value_grad: bfloat16 [16, 8192, 1024], P('dp', 'ctx')
- query_gain_grad: float32 [256], replicated
- key_gain_grad: float32 [256], replicated
Inputs may be any that keep to these rules, and one draw needn't show every extreme that they name: `segment_ids`: in each packed sequence the document numbers never fall along the positions; every document holds 1 to 512 positions and one holds exactly 512.
All inputs are finite; a program needn't handle non-finite values.
Results may differ from a plain program's by a relative error of at most 0.0081.
Values may be sent and summed in bfloat16 or wider, within the bound.
A program may use at most 32 MiB of HBM per device.

v0:
```python
import jax
import jax.numpy as jnp
from jax import lax
from jax.sharding import PartitionSpec as P

HEADS = 8
KV_HEADS = 4
HEAD_DIM = 256
GREACH = 4


epsilon = 1e-06


def from_behind(array, axis, by):
    size = lax.axis_size(axis)
    pairs = [(i, i + by) for i in range(size) if 0 <= i + by < size]
    return lax.ppermute(array, axis, pairs)


def normalize(field, gain_vec):
    as_float = field.astype(jnp.float32)
    inverse = lax.rsqrt(jnp.mean(as_float * as_float, -1, keepdims=True) + epsilon)
    normed = as_float * inverse
    return (normed, inverse, normed * gain_vec)


def norm_backward(upstream, normed, inverse, gain_vec):
    scaled = upstream * gain_vec
    grad_in = inverse * (scaled - normed * jnp.mean(scaled * normed, -1, keepdims=True))
    return (grad_in, jnp.sum(upstream * normed, axis=(0, 1)))


def front_row(field):
    return jnp.concatenate(
        [jnp.zeros((field.shape[0], 1, field.shape[2]), field.dtype), field], axis=1
    )


def shards(segment_ids, queries, keys, values, query_gain, key_gain, out_grad):
    tok_rows = queries.shape[1]
    groups = HEADS // KV_HEADS
    kv_width = KV_HEADS * HEAD_DIM
    reach_rows = GREACH * tok_rows
    position = lax.axis_index("ctx")
    q_normed, q_inverse, q_gained = normalize(
        queries[0].reshape(tok_rows, HEADS, HEAD_DIM), query_gain
    )
    q_scaled = (q_gained * HEAD_DIM ** (-0.5)).astype(jnp.bfloat16)
    k_normed, k_inverse, k_gained = normalize(
        keys[0].reshape(tok_rows, KV_HEADS, HEAD_DIM), key_gain
    )
    own_block = jnp.stack([k_gained.astype(jnp.bfloat16).reshape(tok_rows, kv_width), values[0]])
    earlier = []
    for distance in range(1, GREACH + 1):
        outgoing = own_block if distance < GREACH else own_block[:, 1:]
        arrived = from_behind(outgoing, "ctx", distance)
        earlier.append(arrived if distance < GREACH else front_row(arrived))
    key_band = jnp.concatenate(earlier[::-1] + [own_block], axis=1)
    band_keys = key_band[0].reshape(-1, KV_HEADS, HEAD_DIM)
    band_values = key_band[1].reshape(-1, KV_HEADS, HEAD_DIM)
    seg_row = segment_ids[0]
    seg_padded = jnp.concatenate([jnp.full((reach_rows,), -1, jnp.int32), seg_row])
    first_row = position * tok_rows
    key_seg = lax.dynamic_slice_in_dim(seg_padded, first_row, reach_rows + tok_rows)
    query_seg = lax.dynamic_slice_in_dim(seg_row, first_row, tok_rows)
    column_ids = jnp.arange(reach_rows + tok_rows)[None, :]
    row_ids = jnp.arange(tok_rows)[:, None]
    in_window = (column_ids <= row_ids + reach_rows) & (column_ids > row_ids)
    live_mask = (query_seg[:, None] == key_seg[None, :]) & in_window
    q_heads = q_scaled.reshape(tok_rows, KV_HEADS, groups, HEAD_DIM).transpose(1, 2, 0, 3)
    grad_heads = out_grad[0].reshape(tok_rows, KV_HEADS, groups, HEAD_DIM).transpose(1, 2, 0, 3)
    scores = jnp.einsum("kgid,jkd->kgij", q_heads, band_keys, preferred_element_type=jnp.float32)
    weights = jnp.where(live_mask, jnp.exp(scores), 0.0)
    probs = weights / jnp.sum(weights, -1, keepdims=True)
    probs_low = probs.astype(jnp.bfloat16)
    attended = jnp.einsum(
        "kgij,jkd->ikgd", probs_low, band_values, preferred_element_type=jnp.float32
    )
    attended = attended.astype(jnp.bfloat16).reshape(1, tok_rows, HEADS * HEAD_DIM)
    dprob = jnp.einsum(
        "kgid,jkd->kgij", grad_heads, band_values, preferred_element_type=jnp.float32
    )
    centre = jnp.sum(probs * dprob, -1, keepdims=True)
    dscore = (probs * (dprob - centre)).astype(jnp.bfloat16)
    dq_scaled = jnp.einsum("kgij,jkd->ikgd", dscore, band_keys, preferred_element_type=jnp.float32)
    dq_scaled = dq_scaled.reshape(tok_rows, HEADS, HEAD_DIM)
    key_parts = jnp.einsum("kgij,kgid->kjd", dscore, q_heads, preferred_element_type=jnp.float32)
    value_parts = jnp.einsum(
        "kgij,kgid->kjd", probs_low, grad_heads, preferred_element_type=jnp.float32
    )
    grad_parts = jnp.stack(
        [
            key_parts.astype(jnp.bfloat16).transpose(1, 0, 2).reshape(-1, kv_width),
            value_parts.astype(jnp.bfloat16).transpose(1, 0, 2).reshape(-1, kv_width),
        ]
    )

    def portion(distance):
        return grad_parts[:, (GREACH - distance) * tok_rows : (GREACH - distance + 1) * tok_rows]

    summed = lax.optimization_barrier(portion(0)).astype(jnp.float32)
    for distance in range(1, GREACH + 1):
        outgoing = portion(distance) if distance < GREACH else portion(distance)[:, 1:]
        arrived = from_behind(outgoing, "ctx", -distance)
        if distance == GREACH:
            arrived = front_row(arrived)
        summed = summed + arrived.astype(jnp.float32)
    dk_rounded = summed[0].reshape(tok_rows, KV_HEADS, HEAD_DIM)
    value_grad = summed[1].astype(jnp.bfloat16).reshape(1, tok_rows, kv_width)
    query_grad, query_gain_part = norm_backward(
        dq_scaled * HEAD_DIM ** (-0.5), q_normed, q_inverse, query_gain
    )
    key_grad, key_gain_part = norm_backward(dk_rounded, k_normed, k_inverse, key_gain)
    query_gain_sum, key_gain_sum = lax.psum((query_gain_part, key_gain_part), ("dp", "ctx"))
    factor = (lax.axis_size("dp") * queries.shape[0] * lax.axis_size("ctx") * tok_rows) ** (-0.5)
    return (
        attended,
        query_grad.astype(jnp.bfloat16).reshape(1, tok_rows, HEADS * HEAD_DIM),
        key_grad.astype(jnp.bfloat16).reshape(1, tok_rows, kv_width),
        value_grad,
        query_gain_sum * factor,
        key_gain_sum * factor,
    )


def solution(mesh):
    placed = (
        P("dp", None),
        P("dp", "ctx", None),
        P("dp", "ctx", None),
        P("dp", "ctx", None),
        P(),
        P(),
        P("dp", "ctx", None),
    )
    return jax.shard_map(
        shards,
        mesh=mesh,
        in_specs=placed,
        out_specs=(
            P("dp", "ctx", None),
            P("dp", "ctx", None),
            P("dp", "ctx", None),
            P("dp", "ctx", None),
            P(),
            P(),
        ),
        check_vma=False,
    )
```

profile of v0, /device:TPU:1, one launch (start us, length us, event | category | flops | bytes accessed | tf_op | source)
XLA Modules:
  0.0 319.8 jit_solution(11551383122719071129)
XLA Ops:
  0.6 1.2 copy.86
  1.8 0.7 broadcast_bitcast_fusion.1
  2.5 0.8 multiply_reduce_fusion.2
  3.4 1.1 copy.87
  4.5 0.2 multiply_convert_fusion.2
  4.7 0.1 pad_maximum_fusion
  4.8 0.0 copy-start.5
  4.8 7.1 %collective-permute-start.1 = (bf16[2,128,1024]{1,2,0:T(8,128)(2,1)S(1)}, bf16[2,128,1024]{1,2,0:T(8,128)(2,1)}, u32[]{:S(2)}, u32[]{:S(2)}) collective-permute-start(bf16[2,128,1024]{1,2,0:T(8,128)(2,1)S(1)} %pad_maximum_fusion), channel_id=1, source_target_pairs={{0,3},{1,4},{2,5},{3,6},{4,7},{5,8},{6,9},{7,10},{8,11},{9,12},{10... | collective-permute-start | bytes 1572872 | tf_op jit(solution)/shard_map/ppermute | solution.py:18
  11.9 3.5 %collective-permute-start.2 = (bf16[2,128,1024]{1,2,0:T(8,128)(2,1)S(1)}, bf16[2,128,1024]{1,2,0:T(8,128)(2,1)}, u32[]{:S(2)}, u32[]{:S(2)}) collective-permute-start(bf16[2,128,1024]{1,2,0:T(8,128)(2,1)S(1)} %pad_maximum_fusion), channel_id=1, source_target_pairs={{0,2},{1,3},{2,4},{3,5},{4,6},{5,7},{6,8},{7,9},{8,10},{9,11},{10,... | collective-permute-start | bytes 1572872 | tf_op jit(solution)/shard_map/ppermute | solution.py:18
  15.4 1.9 collective-permute-start.3
  17.3 1.0 fusion.11
  18.3 6.4 %collective-permute-start = (bf16[2,127,1024]{1,2,0:T(8,128)(2,1)}, bf16[2,127,1024]{1,2,0:T(8,128)(2,1)}, u32[]{:S(2)}, u32[]{:S(2)}) collective-permute-start(bf16[2,127,1024]{1,2,0:T(8,128)(2,1)} %fusion.11), channel_id=1, source_target_pairs={{0,4},{1,5},{2,6},{3,7},{4,8},{5,9},{6,10},{7,11},{8,12},{9,13},{1... | collective-permute-start | bytes 1560584 | tf_op jit(solution)/shard_map/ppermute | solution.py:18
  24.7 0.0 copy-done.1
  24.7 1.2 copy.88
  26.0 0.1 convert_multiply_fusion
  26.1 0.3 copy.117
  26.4 0.0 copy-start.8
  26.5 0.0 copy-start.7
  26.5 0.2 reduce_sum.80
  26.7 0.1 copy.92
  26.9 0.2 mul.213
  27.1 1.1 mul.214
  28.2 2.1 copy.115
  30.3 0.1 pad_dynamic-slice_fusion
  30.4 0.2 fusion.20
  30.6 16.8 %collective-permute-done = bf16[2,127,1024]{1,2,0:T(8,128)(2,1)} collective-permute-done((bf16[2,127,1024]{1,2,0:T(8,128)(2,1)}, bf16[2,127,1024]{1,2,0:T(8,128)(2,1)}, u32[]{:S(2)}, u32[]{:S(2)}) %collective-permute-start) | collective-permute-done | bytes 520224 | tf_op jit(solution)/shard_map/ppermute | solution.py:18
  47.4 0.0 collective-permute-done.1
  47.4 0.0 collective-permute-done.2
  47.4 0.0 collective-permute-done.3
  47.4 0.9 broadcast.135
  48.3 4.4 %concatenate.9 = bf16[2,640,1024]{1,2,0:T(8,128)(2,1)S(1)} concatenate(bf16[2,1,1024]{1,2,0:T(8,128)(2,1)} %broadcast.135, bf16[2,127,1024]{1,2,0:T(8,128)(2,1)} %collective-permute-done, bf16[2,128,1024]{1,2,0:T(8,128)(2,1)} %collective-permute-done.1, bf16[2,128,1024]{1,2,0:T(8,128)(2,1)} %collective-permute-done.2, bf16[2,128,1024]{1,2,0:T(8,128)(2,1)} %collective-permute-done.3, ...), dimensions={1} | concatenate | bytes 5242880 | tf_op jit(solution)/shard_map/concatenate | solution.py:59
  52.8 0.2 fusion.26
  53.0 1.0 copy-done
  54.0 0.9 fusion.4
  54.9 0.9 convolution_convert_fusion
  55.7 0.2 copy-done.6
  55.9 1.1 fusion
  57.0 0.7 fusion.2
  57.7 1.7 fusion.6
  59.4 0.6 bitcast_convert_fusion.1
  60.0 0.8 bitcast_convert_fusion
  60.8 1.2 fusion.15
  62.0 1.0 pad_maximum_fusion.1
  63.1 1.0 copy.99
  64.1 0.1 copy.98
  64.2 0.2 mul.227
  64.4 1.1 mul.228
  65.5 2.6 copy.97
  68.2 1.3 collective-permute-start.6
  69.5 1.3 collective-permute-start.5
  70.8 6.0 %collective-permute-start.4 = (bf16[2,128,1024]{1,2,0:T(8,128)(2,1)}, bf16[2,128,1024]{1,2,0:T(8,128)(2,1)S(1)}, u32[]{:S(2)}, u32[]{:S(2)}) collective-permute-start(bf16[2,128,1024]{1,2,0:T(8,128)(2,1)} %get-tuple-element.49), channel_id=1, source_target_pairs={{1,0},{2,1},{3,2},{4,3},{5,4},{6,5},{7,6},{8,7},{9,8},{10,9},{11,1... | collective-permute-start | bytes 1572872 | tf_op jit(solution)/shard_map/ppermute | solution.py:18
  76.7 1.3 collective-permute-start.7
  78.0 2.3 multiply_convert_fusion
  80.4 56.9 %collective-permute-done.7 = bf16[2,127,1024]{1,2,0:T(8,128)(2,1)S(1)} collective-permute-done((bf16[2,127,1024]{1,2,0:T(8,128)(2,1)}, bf16[2,127,1024]{1,2,0:T(8,128)(2,1)S(1)}, u32[]{:S(2)}, u32[]{:S(2)}) %collective-permute-start.7) | collective-permute-done | bytes 520224 | tf_op jit(solution)/shard_map/ppermute | solution.py:18
  137.3 0.0 collective-permute-done.6
  137.3 0.0 collective-permute-done.5
  137.3 0.0 collective-permute-done.4
  137.3 0.4 convert_add_fusion
  137.8 0.1 multiply_reduce_fusion.1
  137.9 0.4 multiply_reduce_fusion
  138.3 0.9 copy.100
  139.2 0.8 copy.101
  140.1 179.2 %all-reduce.2 = (f32[256]{0:T(256)S(1)}, f32[256]{0:T(256)S(1)}) all-reduce(f32[256]{0:T(256)S(1)} %get-tuple-element.42, f32[256]{0:T(256)S(1)} %reduce_sum.88), channel_id=1, replica_groups=mesh['dp'=16,'ctx'=64] {'dp','ctx'}, use_global_device_ids=true, to_apply=%region_7.8 | all-reduce | flops 512 | bytes 4096 | tf_op jit(solution)/shard_map/psum | solution.py:115
  319.3 0.6 broadcast_multiply_fusion.2
  (29 shorter events, 0.2 us)
Async XLA Ops:
  0.6 24.1 %copy-start.1 = (bf16[1,128,2048]{2,1,0:T(8,128)(2,1)S(1)}, bf16[1,128,2048]{2,1,0:T(8,128)(2,1)}, u32[]{:S(2)}) copy-start(bf16[1,128,2048]{2,1,0:T(8,128)(2,1)} %param.8) | copy-start | bytes 1572868
  4.8 21.7 %copy-start.5 = (bf16[2,128,1024]{1,2,0:T(8,128)(2,1)}, bf16[2,128,1024]{1,2,0:T(8,128)(2,1)S(1)}, u32[]{:S(2)}) copy-start(bf16[2,128,1024]{1,2,0:T(8,128)(2,1)S(1)} %pad_maximum_fusion) | copy-start | bytes 1572868
  4.8 42.6 %collective-permute-start.1 = (bf16[2,128,1024]{1,2,0:T(8,128)(2,1)S(1)}, bf16[2,128,1024]{1,2,0:T(8,128)(2,1)}, u32[]{:S(2)}, u32[]{:S(2)}) collective-permute-start(bf16[2,128,1024]{1,2,0:T(8,128)(2,1)S(1)} %pad_maximum_fusion), channel_id=1, source_target_pairs={{0,3},{1,4},{2,5},{3,6},{4,7},{5,8},{6,9},{7,10},{8,11},{9,12},{10... | collective-permute-start | bytes 1572872 | tf_op jit(solution)/shard_map/ppermute | solution.py:18
  11.9 35.6 %collective-permute-start.2 = (bf16[2,128,1024]{1,2,0:T(8,128)(2,1)S(1)}, bf16[2,128,1024]{1,2,0:T(8,128)(2,1)}, u32[]{:S(2)}, u32[]{:S(2)}) collective-permute-start(bf16[2,128,1024]{1,2,0:T(8,128)(2,1)S(1)} %pad_maximum_fusion), channel_id=1, source_target_pairs={{0,2},{1,3},{2,4},{3,5},{4,6},{5,7},{6,8},{7,9},{8,10},{9,11},{10,... | collective-permute-start | bytes 1572872 | tf_op jit(solution)/shard_map/ppermute | solution.py:18
  15.4 32.0 %collective-permute-start.3 = (bf16[2,128,1024]{1,2,0:T(8,128)(2,1)S(1)}, bf16[2,128,1024]{1,2,0:T(8,128)(2,1)}, u32[]{:S(2)}, u32[]{:S(2)}) collective-permute-start(bf16[2,128,1024]{1,2,0:T(8,128)(2,1)S(1)} %pad_maximum_fusion), channel_id=1, source_target_pairs={{0,1},{1,2},{2,3},{3,4},{4,5},{5,6},{6,7},{7,8},{8,9},{9,10},{10,1... | collective-permute-start | bytes 1572872 | tf_op jit(solution)/shard_map/ppermute | solution.py:18
  18.3 29.1 %collective-permute-start = (bf16[2,127,1024]{1,2,0:T(8,128)(2,1)}, bf16[2,127,1024]{1,2,0:T(8,128)(2,1)}, u32[]{:S(2)}, u32[]{:S(2)}) collective-permute-start(bf16[2,127,1024]{1,2,0:T(8,128)(2,1)} %fusion.11), channel_id=1, source_target_pairs={{0,4},{1,5},{2,6},{3,7},{4,8},{5,9},{6,10},{7,11},{8,12},{9,13},{1... | collective-permute-start | bytes 1560584 | tf_op jit(solution)/shard_map/ppermute | solution.py:18
  26.4 1.8 copy-start.8
  26.5 3.9 %copy-start.7 = (s32[1,8192]{1,0:T(1,128)S(1)}, s32[1,8192]{1,0:T(1,128)}, u32[]{:S(2)}) copy-start(s32[1,8192]{1,0:T(1,128)} %param.7) | copy-start | bytes 98308
  52.8 1.2 copy-start
  54.9 1.0 copy-start.6
  64.2 13.8 %copy-start.2 = (f32[1,128,2048]{2,1,0:T(8,128)S(1)}, f32[1,128,2048]{2,1,0:T(8,128)}, u32[]{:S(2)}) copy-start(f32[1,128,2048]{2,1,0:T(8,128)} %mul.214) | copy-start | bytes 3145732
  65.5 12.5 %copy-start.3 = (f32[1,128,2048]{2,1,0:T(8,128)S(1)}, f32[1,128,2048]{2,1,0:T(8,128)}, u32[]{:S(2)}) copy-start(f32[1,128,2048]{2,1,0:T(8,128)} %mul.228) | copy-start | bytes 3145732
  68.2 69.1 %collective-permute-start.6 = (bf16[2,128,1024]{1,2,0:T(8,128)(2,1)}, bf16[2,128,1024]{1,2,0:T(8,128)(2,1)S(1)}, u32[]{:S(2)}, u32[]{:S(2)}) collective-permute-start(bf16[2,128,1024]{1,2,0:T(8,128)(2,1)} %get-tuple-element.51), channel_id=1, source_target_pairs={{3,0},{4,1},{5,2},{6,3},{7,4},{8,5},{9,6},{10,7},{11,8},{12,9},{13... | collective-permute-start | bytes 1572872 | tf_op jit(solution)/shard_map/ppermute | solution.py:18
  69.5 67.8 %collective-permute-start.5 = (bf16[2,128,1024]{1,2,0:T(8,128)(2,1)}, bf16[2,128,1024]{1,2,0:T(8,128)(2,1)S(1)}, u32[]{:S(2)}, u32[]{:S(2)}) collective-permute-start(bf16[2,128,1024]{1,2,0:T(8,128)(2,1)} %get-tuple-element.50), channel_id=1, source_target_pairs={{2,0},{3,1},{4,2},{5,3},{6,4},{7,5},{8,6},{9,7},{10,8},{11,9},{12,... | collective-permute-start | bytes 1572872 | tf_op jit(solution)/shard_map/ppermute | solution.py:18
  70.8 66.5 %collective-permute-start.4 = (bf16[2,128,1024]{1,2,0:T(8,128)(2,1)}, bf16[2,128,1024]{1,2,0:T(8,128)(2,1)S(1)}, u32[]{:S(2)}, u32[]{:S(2)}) collective-permute-start(bf16[2,128,1024]{1,2,0:T(8,128)(2,1)} %get-tuple-element.49), channel_id=1, source_target_pairs={{1,0},{2,1},{3,2},{4,3},{5,4},{6,5},{7,6},{8,7},{9,8},{10,9},{11,1... | collective-permute-start | bytes 1572872 | tf_op jit(solution)/shard_map/ppermute | solution.py:18
  76.7 60.6 %collective-permute-start.7 = (bf16[2,127,1024]{1,2,0:T(8,128)(2,1)}, bf16[2,127,1024]{1,2,0:T(8,128)(2,1)S(1)}, u32[]{:S(2)}, u32[]{:S(2)}) collective-permute-start(bf16[2,127,1024]{1,2,0:T(8,128)(2,1)} %pad_maximum_fusion.1), channel_id=1, source_target_pairs={{4,0},{5,1},{6,2},{7,3},{8,4},{9,5},{10,6},{11,7},{12,8},{13,9},{1... | collective-permute-start | bytes 1560584 | tf_op jit(solution)/shard_map/ppermute | solution.py:18
  80.4 57.4 %copy-start.4 = (f32[128,4,256]{0,2,1:T(8,128)S(1)}, f32[128,4,256]{0,2,1:T(8,128)}, u32[]{:S(2)}) copy-start(f32[128,4,256]{0,2,1:T(8,128)} %get-tuple-element.47) | copy-start | bytes 1572868
  80.4 57.4 %copy-start.9 = (f32[256]{0:T(256)S(1)}, f32[256]{0:T(256)}, u32[]{:S(2)}) copy-start(f32[256]{0:T(256)} %param.12) | copy-start | bytes 3076
where the time goes:
time: 321 us; the launch traced here: 320 us
  blocking collectives  179 us (56%)
  waiting for transfers between devices  73.8 us (23%)
  starting transfers between devices  28.7 us (9%)
  local copies, waits for them, and re-layouts  21.8 us (7%)
  other arithmetic  9.38 us (3%)
  matrix products  5.95 us (2%)
    psum x1, blocking collectives, shards(): lax.psum((query_gain_part, key_gain_part), ('dp', 'ctx'))  179 us
    ppermute x8, waiting for transfers between devices, from_behind(): return lax.ppermute(array, axis, pairs)  73.8 us
    ppermute x8, starting transfers between devices, from_behind(): return lax.ppermute(array, axis, pairs)  28.7 us
    unnamed x30, local copies, waits for them, and re-layouts  7.24 us
  transfers between devices with their start and end apart: 8, of which 2 were waited for; matrix products, arithmetic and copies ran while one was open for 3% of the time, Pallas kernels for 0%

commit v1 on v0

v1 whole, which is shorter than its diff:
```python
import jax
import jax.numpy as jnp
from jax import lax
from jax.experimental import pallas as pl
from jax.experimental.pallas import tpu as pltpu
from jax.sharding import PartitionSpec as P

HEADS = 8
KV_HEADS = 4
GROUPS = HEADS // KV_HEADS
HEAD_DIM = 256
TOK = 128
GREACH = 4
BAND = GREACH + 1
ROWS = GROUPS * TOK
SIDE = 4
EPSILON = 1e-06
SCALE = HEAD_DIM ** (-0.5)

MESH = pl.DeviceIdType.MESH
F32 = jnp.float32
BF16 = jnp.bfloat16

NEXT, RELAY, NEAR, FAR = range(4)


def wrap(value, size):
    return lax.rem(value + size, size)


def dot_nt(a, b):
    return lax.dot_general(a, b, (((1,), (1,)), ((), ())), preferred_element_type=F32)


def dot_tn(a, b):
    return lax.dot_general(a, b, (((0,), (0,)), ((), ())), preferred_element_type=F32)


def dot_nn(a, b):
    return lax.dot_general(a, b, (((1,), (0,)), ((), ())), preferred_element_type=F32)


def inverse_norm(field):
    return lax.rsqrt(jnp.mean(field * field, -1, keepdims=True) + EPSILON)


def norm_backward(upstream, normed, inverse, gain):
    scaled = upstream * gain
    return inverse * (scaled - normed * jnp.mean(scaled * normed, -1, keepdims=True))


def head_columns(head):
    return pl.ds(head * HEAD_DIM, HEAD_DIM)


def kernel(
    ctx_size,
    factor,
    seg_hbm,
    q_hbm,
    k_hbm,
    v_hbm,
    q_gain,
    k_gain,
    g_hbm,
    att_out,
    dq_out,
    dk_out,
    dv_out,
    q_gain_out,
    k_gain_out,
    seg_rows,
    mask,
    q_raw,
    q_scaled,
    out_grad,
    k_raw,
    band,
    part_out,
    part_in,
    kept,
    sum_out,
    sum_in,
    gain_part,
    ar_x,
    ar_y,
    ar_z,
    ar_far,
    ar_core,
    load_sem,
    band_send,
    band_recv,
    part_send,
    part_recv,
    sum_send,
    sum_recv,
    ar_send,
    ar_recv,
    known,
):
    dp = lax.axis_index("dp")
    me = lax.axis_index("ctx")
    core = lax.rem(me, 2)
    z = lax.div(me, 2)
    x = lax.rem(dp, SIDE)
    y = lax.div(dp, SIDE)
    chips = ctx_size // 2

    partner = (dp, me + 1 - 2 * core)

    def along_z(step):
        return (dp, wrap(me + 2 * step, ctx_size))

    def along_x(step):
        return (y * SIDE + wrap(x + step, SIDE), me)

    def along_y(step):
        return (wrap(y + step, SIDE) * SIDE + x, me)

    ahead = along_z(1)
    behind = along_z(-1)

    loads = {}

    def load(name, slot, source, target):
        copy = pltpu.make_async_copy(source, target, load_sem.at[slot])
        copy.start()
        loads[name] = copy

    for head in range(KV_HEADS):
        load(("k", head), head, k_hbm.at[0, :, head_columns(head)], k_raw.at[head])
        load(("v", head), 4 + head, v_hbm.at[0, :, head_columns(head)], band.at[head, 0, 1])
    for distance in range(BAND):
        first = pl.multiple_of(jnp.maximum(me - distance, 0) * TOK, TOK)
        load(("s", distance), 24 + distance, seg_hbm.at[:, pl.ds(first, TOK)], seg_rows.at[distance])
    for head in range(HEADS):
        rows = pl.ds((head % GROUPS) * TOK, TOK)
        load(("q", head), 8 + head, q_hbm.at[0, :, head_columns(head)], q_raw.at[head])
        load(
            ("g", head),
            16 + head,
            g_hbm.at[0, :, head_columns(head)],
            out_grad.at[head // GROUPS, rows],
        )

    nearby = [along_z(1), along_z(-1), along_x(1), along_x(-1), along_y(1), along_y(-1)]
    barrier = pltpu.get_barrier_semaphore()
    for device in nearby + [partner]:
        pl.semaphore_signal(barrier, inc=1, device_id=device, device_id_type=MESH)

    def remote(source, target, send, recv, device):
        return pltpu.make_async_remote_copy(
            src_ref=source,
            dst_ref=target,
            send_sem=send,
            recv_sem=recv,
            device_id=device,
            device_id_type=MESH,
        )

    def band_copy(head, kind):
        source, target, device = {
            NEXT: (0, 2, ahead),
            RELAY: (2, 4, ahead),
            NEAR: (2 * core, 1, partner),
            FAR: (2 + 2 * core, 3, partner),
        }[kind]
        return remote(
            band.at[head, source],
            band.at[head, target],
            band_send.at[head, kind],
            band_recv.at[head, kind],
            device,
        )

    def part_copy(head):
        return remote(
            part_out.at[head], part_in.at[head], part_send.at[head], part_recv.at[head], partner
        )

    def sum_copy(head, stage):
        return remote(
            sum_out.at[head, stage],
            sum_in.at[head, stage],
            sum_send.at[head, stage],
            sum_recv.at[head, stage],
            behind,
        )

    def tell(stage, devices):
        for device in devices:
            pl.semaphore_signal(known.at[stage], inc=1, device_id=device, device_id_type=MESH)

    def hear(stage, count):
        pl.semaphore_wait(known.at[stage], count)

    def key_normed(head):
        field = k_raw[head].astype(F32)
        inverse = inverse_norm(field)
        return field * inverse, inverse

    def query_normed(head):
        field = q_raw[head].astype(F32)
        inverse = inverse_norm(field)
        return field * inverse, inverse

    def prepare_keys(head):
        loads["k", head].wait()
        normed, _ = key_normed(head)
        band[head, 0, 0] = (normed * k_gain[...]).astype(BF16)
        loads["v", head].wait()

    def prepare_queries(kv_head):
        for group in range(GROUPS):
            head = kv_head * GROUPS + group
            loads["q", head].wait()
            normed, _ = query_normed(head)
            q_scaled[kv_head, pl.ds(group * TOK, TOK)] = (normed * q_gain[...] * SCALE).astype(BF16)
            loads["g", head].wait()

    def prepare_mask():
        for distance in range(BAND):
            loads["s", distance].wait()
        query_seg = seg_rows[0].astype(F32)
        key_at = lax.broadcasted_iota(jnp.int32, (TOK, TOK), 0)
        query_at = lax.broadcasted_iota(jnp.int32, (TOK, TOK), 1)
        for distance in range(BAND):
            key_seg = jnp.where(me >= distance, seg_rows[distance].astype(F32), -1.0)
            key_column = jnp.broadcast_to(key_seg, (TOK, TOK)).T
            live = key_column == query_seg
            if distance == 0:
                live = live & (key_at <= query_at)
            if distance == GREACH:
                live = live & (key_at > query_at)
            weight = jnp.where(live, 1.0, 0.0)
            for group in range(GROUPS):
                mask[distance, :, pl.ds(group * TOK, TOK)] = weight

    def attend(head):
        queries = q_scaled[head]
        grads = out_grad[head]
        weights, dprobs = {}, {}
        total = jnp.zeros((1, ROWS), F32)
        weighted = jnp.zeros((1, ROWS), F32)
        for distance in range(BAND):
            weight = jnp.exp(dot_nt(band[head, distance, 0], queries)) * mask[distance]
            dprob = dot_nt(band[head, distance, 1], grads)
            total = total + jnp.sum(weight, 0, keepdims=True)
            weighted = weighted + jnp.sum(weight * dprob, 0, keepdims=True)
            weights[distance], dprobs[distance] = weight, dprob
        inverse = 1.0 / total
        centre = weighted * inverse
        attended = jnp.zeros((ROWS, HEAD_DIM), F32)
        dq_scaled = jnp.zeros((ROWS, HEAD_DIM), F32)
        for distance in (1, 3, 4, 2, 0):
            probs = weights[distance] * inverse
            dscore = (probs * (dprobs[distance] - centre)).astype(BF16)
            probs = probs.astype(BF16)
            key_part = dot_nn(dscore, queries)
            value_part = dot_nn(probs, grads)
            if distance % 2 == 1:
                part_out[head, distance // 2, 0] = key_part.astype(BF16)
                part_out[head, distance // 2, 1] = value_part.astype(BF16)
            else:
                kept[head, distance // 2, 0] = key_part
                kept[head, distance // 2, 1] = value_part
            attended = attended + dot_tn(probs, band[head, distance, 1])
            dq_scaled = dq_scaled + dot_tn(dscore, band[head, distance, 0])
            if distance == 4:
                part_copy(head).start()
        key_gain_part = jnp.sum(dq_scaled * queries.astype(F32), 0, keepdims=True)
        query_gain_part = jnp.zeros((1, HEAD_DIM), F32)
        for group in range(GROUPS):
            query_head = head * GROUPS + group
            rows = slice(group * TOK, (group + 1) * TOK)
            columns = head_columns(query_head)
            att_out[0, :, columns] = attended[rows].astype(BF16)
            normed, inverse_q = query_normed(query_head)
            upstream = dq_scaled[rows] * SCALE
            query_gain_part = query_gain_part + jnp.sum(upstream * normed, 0, keepdims=True)
            dq = norm_backward(upstream, normed, inverse_q, q_gain[...])
            dq_out[0, :, columns] = dq.astype(BF16)
        both = jnp.concatenate([query_gain_part, key_gain_part], axis=0)
        gain_part[...] = both if head == 0 else gain_part[...] + both

    def send_own(head):
        band_copy(head, NEXT).start()

    def pass_on(head):
        band_copy(head, NEXT).wait_recv()
        band_copy(head, RELAY).start()
        band_copy(head, NEAR).start()

    def share(head):
        band_copy(head, RELAY).wait_recv()
        band_copy(head, FAR).start()

    def band_ready(head):
        band_copy(head, NEAR).wait_recv()
        band_copy(head, FAR).wait_recv()

    def join_parts(head):
        part_copy(head).wait_recv()
        kept[head, core] = kept[head, core] + part_in[head, 0].astype(F32)
        kept[head, core + 1] = kept[head, core + 1] + part_in[head, 1].astype(F32)
        sum_out[head, 0] = kept[head, 2].astype(BF16)
        sum_copy(head, 0).start()

    def pass_back(head):
        sum_copy(head, 0).wait_recv()
        sum_out[head, 1] = (kept[head, 1] + sum_in[head, 0].astype(F32)).astype(BF16)
        sum_copy(head, 1).start()

    def finish_keys(head):
        sum_copy(head, 1).wait_recv()
        dk = kept[head, 0, 0] + sum_in[head, 1, 0].astype(F32)
        dv = kept[head, 0, 1] + sum_in[head, 1, 1].astype(F32)
        dv_out[0, :, head_columns(head)] = dv.astype(BF16)
        normed, inverse = key_normed(head)
        dk = norm_backward(dk, normed, inverse, k_gain[...])
        dk_out[0, :, head_columns(head)] = dk.astype(BF16)

    def ar_copies(stage, buffer, mine, size, device_of):
        sends, arrivals = [], []
        for step in range(1, size):
            other = wrap(mine + step, size)
            device = device_of(other)
            send = ar_send.at[stage, step]
            sends.append(remote(buffer.at[mine], buffer.at[mine], send, ar_recv.at[stage, mine], device))
            arrivals.append(remote(buffer.at[other], buffer.at[other], send, ar_recv.at[stage, other], device))
        return sends, arrivals

    def ar_start(stage, buffer, mine, size, device_of, value):
        buffer[mine] = value
        sends, arrivals = ar_copies(stage, buffer, mine, size, device_of)
        for copy in sends:
            copy.start()

        def finish():
            for copy in arrivals:
                copy.wait_recv()
            for copy in sends:
                copy.wait_send()
            total = buffer[0]
            for slot in range(1, size):
                total = total + buffer[slot]
            return total

        return finish

    quad = lax.div(z, SIDE)
    in_quad = lax.rem(z, SIDE)

    prepare_keys(0)
    pl.semaphore_wait(barrier, len(nearby) + 1)
    send_own(0)
    tell(0, nearby)
    prepare_keys(1)
    send_own(1)
    prepare_keys(2)
    prepare_keys(3)
    prepare_queries(0)
    hear(0, len(nearby))
    tell(1, [along_z(2), along_z(-2)])
    prepare_mask()
    pass_on(0)
    send_own(2)
    prepare_queries(1)
    hear(1, 2)
    tell(2, [along_z(4), along_z(-4)])
    pass_on(1)
    send_own(3)
    prepare_queries(2)
    prepare_queries(3)
    share(0)
    band_ready(0)
    attend(0)
    hear(2, 2)
    tell(3, [along_z(8), along_z(-8)])
    pass_on(2)
    join_parts(0)
    share(1)
    band_ready(1)
    attend(1)
    hear(3, 2)
    pass_on(3)
    join_parts(1)
    pass_back(0)
    share(2)
    band_ready(2)
    attend(2)
    join_parts(2)
    pass_back(1)
    finish_keys(0)
    share(3)
    band_ready(3)
    attend(3)

    finish = ar_start(0, ar_x, x, SIDE, lambda other: (y * SIDE + other, me), gain_part[...])
    join_parts(3)
    pass_back(2)
    finish = ar_start(1, ar_y, y, SIDE, lambda other: (other * SIDE + x, me), finish())
    finish_keys(1)
    finish = ar_start(
        2, ar_z, in_quad, SIDE, lambda other: (dp, (quad * SIDE + other) * 2 + core), finish()
    )
    pass_back(3)
    finish = ar_start(
        3,
        ar_far,
        quad,
        chips // SIDE,
        lambda other: (dp, (other * SIDE + in_quad) * 2 + core),
        finish(),
    )
    finish_keys(2)
    finish_keys(3)
    finish = ar_start(4, ar_core, core, 2, lambda other: partner, finish())
    total = finish() * factor
    q_gain_out[...] = total[0:1]
    k_gain_out[...] = total[1:2] / k_gain[...]

    for head in range(KV_HEADS):
        for kind in range(4):
            band_copy(head, kind).wait_send()
        part_copy(head).wait_send()
        for stage in range(2):
            sum_copy(head, stage).wait_send()


def shards(segment_ids, queries, keys, values, query_gain, key_gain, out_grad):
    ctx_size = lax.axis_size("ctx")
    factor = (lax.axis_size("dp") * queries.shape[0] * ctx_size * queries.shape[1]) ** (-0.5)
    width = KV_HEADS * HEAD_DIM
    hbm = pl.BlockSpec(memory_space=pltpu.HBM)
    vmem = pl.BlockSpec(memory_space=pltpu.VMEM)
    dma = pltpu.SemaphoreType.DMA
    pair = (2, TOK, HEAD_DIM)
    quads = ctx_size // 2 // SIDE
    outs = pl.pallas_call(
        lambda *refs: kernel(ctx_size, factor, *refs),
        out_shape=(
            jax.ShapeDtypeStruct((1, TOK, HEADS * HEAD_DIM), BF16),
            jax.ShapeDtypeStruct((1, TOK, HEADS * HEAD_DIM), BF16),
            jax.ShapeDtypeStruct((1, TOK, width), BF16),
            jax.ShapeDtypeStruct((1, TOK, width), BF16),
            jax.ShapeDtypeStruct((1, HEAD_DIM), F32),
            jax.ShapeDtypeStruct((1, HEAD_DIM), F32),
        ),
        in_specs=[hbm, hbm, hbm, hbm, vmem, vmem, hbm],
        out_specs=(vmem,) * 6,
        scratch_shapes=[
            pltpu.VMEM((BAND, 1, TOK), jnp.int32),
            pltpu.VMEM((BAND, TOK, ROWS), F32),
            pltpu.VMEM((HEADS, TOK, HEAD_DIM), BF16),
            pltpu.VMEM((KV_HEADS, ROWS, HEAD_DIM), BF16),
            pltpu.VMEM((KV_HEADS, ROWS, HEAD_DIM), BF16),
            pltpu.VMEM((KV_HEADS, TOK, HEAD_DIM), BF16),
            pltpu.VMEM((KV_HEADS, BAND) + pair, BF16),
            pltpu.VMEM((KV_HEADS, 2) + pair, BF16),
            pltpu.VMEM((KV_HEADS, 2) + pair, BF16),
            pltpu.VMEM((KV_HEADS, 3) + pair, F32),
            pltpu.VMEM((KV_HEADS, 2) + pair, BF16),
            pltpu.VMEM((KV_HEADS, 2) + pair, BF16),
            pltpu.VMEM((2, HEAD_DIM), F32),
            pltpu.VMEM((SIDE, 2, HEAD_DIM), F32),
            pltpu.VMEM((SIDE, 2, HEAD_DIM), F32),
            pltpu.VMEM((SIDE, 2, HEAD_DIM), F32),
            pltpu.VMEM((quads, 2, HEAD_DIM), F32),
            pltpu.VMEM((2, 2, HEAD_DIM), F32),
            dma((24 + BAND,)),
            dma((KV_HEADS, 4)),
            dma((KV_HEADS, 4)),
            dma((KV_HEADS,)),
            dma((KV_HEADS,)),
            dma((KV_HEADS, 2)),
            dma((KV_HEADS, 2)),
            dma((5, quads)),
            dma((5, quads)),
            pltpu.SemaphoreType.REGULAR((4,)),
        ],
        compiler_params=pltpu.CompilerParams(
            collective_id=0, has_side_effects=True, vmem_limit_bytes=67043328
        ),
    )(
        segment_ids,
        queries,
        keys,
        values,
        query_gain.reshape(1, HEAD_DIM),
        key_gain.reshape(1, HEAD_DIM),
        out_grad,
    )
    return (*outs[:4], outs[4].reshape(HEAD_DIM), outs[5].reshape(HEAD_DIM))


def solution(mesh):
    blocks = P("dp", "ctx", None)
    return jax.shard_map(
        shards,
        mesh=mesh,
        in_specs=(P("dp", None), blocks, blocks, blocks, P(), P(), blocks),
        out_specs=(blocks, blocks, blocks, blocks, P(), P()),
        check_vma=False,
    )
```

time: 321 us -> 87.2 us (0.27)
  blocking collectives: 179 us -> 0 us
  Pallas kernels: 0 us -> 80.2 us
  waiting for transfers between devices: 73.8 us -> 0 us
  starting transfers between devices: 28.7 us -> 0 us
  local copies, waits for them, and re-layouts: 21.8 us -> 6.01 us
  other arithmetic: 9.38 us -> 0 us
  matrix products: 5.95 us -> 0 us
    psum x1 -> x0, blocking collectives: 179 us -> none  [shards(): lax.psum((query_gain_part, key_gain_part), ('dp', 'ctx'))]
    pallas_call x0 -> x1, Pallas kernels: none -> 80.2 us  [shards(): pl.pallas_call(lambda *refs: kernel(ctx_size, factor, *refs), out_shape=(...]
    ppermute x8 -> x0, waiting for transfers between devices: 73.8 us -> none  [from_behind(): return lax.ppermute(array, axis, pairs)]
    ppermute x8 -> x0, starting transfers between devices: 28.7 us -> none  [from_behind(): return lax.ppermute(array, axis, pairs)]
    dot_general x6 -> x0, matrix products: 5.95 us -> none  [the longest x1 1.69 us: shards(): jnp.einsum('kgij,jkd->ikgd', dscore, band_keys, preferred_element_type=jn...]
    concatenate x1 -> x0, local copies, waits for them, and re-layouts: 4.45 us -> none  [shards(): key_band = jnp.concatenate(earlier[::-1] + [own_block], axis=1)]
    another operation x4 -> x0, other arithmetic: 3.32 us -> none  [the longest x2 2.27 us: shards(): jnp.stack([key_parts.astype(jnp.bfloat16).transpose(1, 0, 2).reshape(-1,...]
    unnamed x30 -> x16, local copies, waits for them, and re-layouts: 7.24 us -> 6.01 us
  transfers between devices with their start and end apart: 8 -> 0, of which waited for: 2 -> 0; matrix products, arithmetic and copies ran while one was open for 3% -> 0% of each run, Pallas kernels for 0% -> 0%
where the time goes in v1:
time: 87.2 us; the launch traced here: 86.9 us
  Pallas kernels  80.2 us (92%)
  local copies, waits for them, and re-layouts  6.01 us (7%)
    pallas_call x1, Pallas kernels, shards(): pl.pallas_call(lambda *refs: kernel(ctx_size, factor, *refs), out_shape=(...  80.2 us
    unnamed x16, local copies, waits for them, and re-layouts  6.01 us

profile of v1, /device:TPU:1, one launch (start us, length us, event | category | flops | bytes accessed | tf_op | source)
XLA Modules:
  0.0 86.9 jit_solution(13815528836900394120)
XLA Ops:
  0.6 80.2 %shard_map.118 = (bf16[1,128,2048]{2,1,0:T(8,128)(2,1)}, bf16[1,128,2048]{2,1,0:T(8,128)(2,1)}, bf16[1,128,1024]{2,1,0:T(8,128)(2,1)}, bf16[1,128,1024]{2,1,0:T(...) custom-call(s32[1,8192]{1,0:T(1,128)} %refs_0_.1, bf16[1,128,2048]{2,1,0:T(8,128)(2,1)} %refs_1_.1, ...), custom_call_target="tpu_custom_call" | custom-call | tf_op jit(solution)/shard_map/pallas_call | solution.py:440
  80.9 0.0 copy-start
  80.9 1.9 %copy.19 = bf16[1,128,2048]{2,1,0:T(8,128)(2,1)} copy(bf16[1,128,2048]{2,1,0:T(8,128)(2,1)} %get-tuple-element.24) | data formatting | bytes 1048576
  82.8 0.0 copy-done
  82.8 0.0 copy-start.2
  82.8 0.8 copy.20
  83.6 0.3 copy-done.2
  83.9 0.0 copy-start.1
  83.9 0.7 copy.21
  84.6 0.3 copy-done.1
  85.0 0.0 copy-start.4
  85.0 0.7 copy.22
  85.7 0.0 copy-done.4
  85.7 0.0 copy-start.3
  85.7 0.6 copy.23
  86.2 0.1 copy-done.3
  86.3 0.6 copy.24
Async XLA Ops:
  80.9 2.0 %copy-start = (bf16[1,128,2048]{2,1,0:T(8,128)(2,1)S(1)}, bf16[1,128,2048]{2,1,0:T(8,128)(2,1)}, u32[]{:S(2)}) copy-start(bf16[1,128,2048]{2,1,0:T(8,128)(2,1)} %get-tuple-element.25) | copy-start | bytes 1572868
  82.8 1.1 %copy-start.2 = (bf16[1,128,1024]{2,1,0:T(8,128)(2,1)S(1)}, bf16[1,128,1024]{2,1,0:T(8,128)(2,1)}, u32[]{:S(2)}) copy-start(bf16[1,128,1024]{2,1,0:T(8,128)(2,1)} %get-tuple-element.26) | copy-start | bytes 786436
  83.9 1.0 %copy-start.1 = (bf16[1,128,1024]{2,1,0:T(8,128)(2,1)S(1)}, bf16[1,128,1024]{2,1,0:T(8,128)(2,1)}, u32[]{:S(2)}) copy-start(bf16[1,128,1024]{2,1,0:T(8,128)(2,1)} %get-tuple-element.27) | copy-start | bytes 786436
  85.0 0.7 copy-start.4
  85.7 0.7 copy-start.3

commit v2 on v1

--- a/solution.py
+++ b/solution.py
@@ -21,7 +21,7 @@
 F32 = jnp.float32
 BF16 = jnp.bfloat16
 
-NEXT, RELAY, NEAR, FAR = range(4)
+NEXT, RELAY, NEAR, FAR, FIRST = range(5)
 
 
 def wrap(value, size):
@@ -60,15 +60,17 @@
     q_hbm,
     k_hbm,
     v_hbm,
+    q_gain_hbm,
+    k_gain_hbm,
+    g_hbm,
+    att_hbm,
+    dq_hbm,
+    dk_hbm,
+    dv_hbm,
+    q_gain_grad_hbm,
+    k_gain_grad_hbm,
     q_gain,
     k_gain,
-    g_hbm,
-    att_out,
-    dq_out,
-    dk_out,
-    dv_out,
-    q_gain_out,
-    k_gain_out,
     seg_rows,
     mask,
     q_raw,
@@ -81,13 +83,17 @@
     kept,
     sum_out,
     sum_in,
+    att_buf,
+    dq_buf,
+    dk_buf,
+    dv_buf,
     gain_part,
-    ar_x,
-    ar_y,
+    gain_grads,
+    ar_plane,
     ar_z,
-    ar_far,
     ar_core,
     load_sem,
+    store_sem,
     band_send,
     band_recv,
     part_send,
@@ -120,6 +126,11 @@
     ahead = along_z(1)
     behind = along_z(-1)
 
+    nearby = [along_z(1), along_z(-1), along_x(1), along_x(-1), along_y(1), along_y(-1)]
+    barrier = pltpu.get_barrier_semaphore()
+    for device in nearby + [partner]:
+        pl.semaphore_signal(barrier, inc=1, device_id=device, device_id_type=MESH)
+
     loads = {}
 
     def load(name, slot, source, target):
@@ -127,6 +138,8 @@
         copy.start()
         loads[name] = copy
 
+    load("k_gain", 24 + BAND, k_gain_hbm, k_gain)
+    load("q_gain", 25 + BAND, q_gain_hbm, q_gain)
     for head in range(KV_HEADS):
         load(("k", head), head, k_hbm.at[0, :, head_columns(head)], k_raw.at[head])
         load(("v", head), 4 + head, v_hbm.at[0, :, head_columns(head)], band.at[head, 0, 1])
@@ -143,11 +156,6 @@
             out_grad.at[head // GROUPS, rows],
         )
 
-    nearby = [along_z(1), along_z(-1), along_x(1), along_x(-1), along_y(1), along_y(-1)]
-    barrier = pltpu.get_barrier_semaphore()
-    for device in nearby + [partner]:
-        pl.semaphore_signal(barrier, inc=1, device_id=device, device_id_type=MESH)
-
     def remote(source, target, send, recv, device):
         return pltpu.make_async_remote_copy(
             src_ref=source,
@@ -159,15 +167,21 @@
         )
 
     def band_copy(head, kind):
-        source, target, device = {
+        slot, target, device = {
             NEXT: (0, 2, ahead),
             RELAY: (2, 4, ahead),
             NEAR: (2 * core, 1, partner),
             FAR: (2 + 2 * core, 3, partner),
+            FIRST: (0, 2, ahead),
         }[kind]
+        source, target = band.at[head, slot], band.at[head, target]
+        if kind == FIRST:
+            source, target = v_hbm.at[0, :, head_columns(head)], band.at[head, 2, 1]
+        elif kind == NEXT and head == 0:
+            source, target = band.at[head, 0, 0], band.at[head, 2, 0]
         return remote(
-            band.at[head, source],
-            band.at[head, target],
+            source,
+            target,
             band_send.at[head, kind],
             band_recv.at[head, kind],
             device,
@@ -236,68 +250,91 @@
             for group in range(GROUPS):
                 mask[distance, :, pl.ds(group * TOK, TOK)] = weight
 
-    def attend(head):
+    stores = []
+
+    def store(slot, source, target):
+        copy = pltpu.make_async_copy(source, target, store_sem.at[slot])
+        copy.start()
+        stores.append(copy)
+
+    def score(head, distances, state):
+        total, weighted, weights, dprobs = state
         queries = q_scaled[head]
         grads = out_grad[head]
-        weights, dprobs = {}, {}
-        total = jnp.zeros((1, ROWS), F32)
-        weighted = jnp.zeros((1, ROWS), F32)
-        for distance in range(BAND):
+        for distance in distances:
             weight = jnp.exp(dot_nt(band[head, distance, 0], queries)) * mask[distance]
             dprob = dot_nt(band[head, distance, 1], grads)
             total = total + jnp.sum(weight, 0, keepdims=True)
             weighted = weighted + jnp.sum(weight * dprob, 0, keepdims=True)
-            weights[distance], dprobs[distance] = weight, dprob
+            weights = weights | {distance: weight}
+            dprobs = dprobs | {distance: dprob}
+        return total, weighted, weights, dprobs
+
+    def begin(head):
+        band_copy(head, NEAR).wait_recv()
+        zero = jnp.zeros((1, ROWS), F32)
+        return score(head, (0, 2, 1), (zero, zero, {}, {}))
+
+    def attend(head, state, after_gains=None):
+        band_copy(head, FAR).wait_recv()
+        total, weighted, weights, dprobs = score(head, (4, 3), state)
+        queries = q_scaled[head]
+        grads = out_grad[head]
         inverse = 1.0 / total
         centre = weighted * inverse
-        attended = jnp.zeros((ROWS, HEAD_DIM), F32)
+        probs, dscores = {}, {}
         dq_scaled = jnp.zeros((ROWS, HEAD_DIM), F32)
-        for distance in (1, 3, 4, 2, 0):
-            probs = weights[distance] * inverse
-            dscore = (probs * (dprobs[distance] - centre)).astype(BF16)
-            probs = probs.astype(BF16)
-            key_part = dot_nn(dscore, queries)
-            value_part = dot_nn(probs, grads)
-            if distance % 2 == 1:
-                part_out[head, distance // 2, 0] = key_part.astype(BF16)
-                part_out[head, distance // 2, 1] = value_part.astype(BF16)
-            else:
-                kept[head, distance // 2, 0] = key_part
-                kept[head, distance // 2, 1] = value_part
-            attended = attended + dot_tn(probs, band[head, distance, 1])
-            dq_scaled = dq_scaled + dot_tn(dscore, band[head, distance, 0])
-            if distance == 4:
-                part_copy(head).start()
+        for distance in range(BAND):
+            prob = weights[distance] * inverse
+            dscores[distance] = (prob * (dprobs[distance] - centre)).astype(BF16)
+            probs[distance] = prob.astype(BF16)
+            dq_scaled = dq_scaled + dot_tn(dscores[distance], band[head, distance, 0])
         key_gain_part = jnp.sum(dq_scaled * queries.astype(F32), 0, keepdims=True)
         query_gain_part = jnp.zeros((1, HEAD_DIM), F32)
         for group in range(GROUPS):
+            normed, _ = query_normed(head * GROUPS + group)
+            upstream = dq_scaled[group * TOK : (group + 1) * TOK] * SCALE
+            query_gain_part = query_gain_part + jnp.sum(upstream * normed, 0, keepdims=True)
+        both = jnp.concatenate([query_gain_part, key_gain_part], axis=0)
+        gain_part[...] = both if head == 0 else gain_part[...] + both
+        later = after_gains() if after_gains else None
+        for distance in (1, 3):
+            key_part = dot_nn(dscores[distance], queries)
+            value_part = dot_nn(probs[distance], grads)
+            part_out[head, distance // 2, 0] = key_part.astype(BF16)
+            part_out[head, distance // 2, 1] = value_part.astype(BF16)
+        attended = jnp.zeros((ROWS, HEAD_DIM), F32)
+        for distance in (4, 2, 0):
+            kept[head, distance // 2, 0] = dot_nn(dscores[distance], queries)
+            kept[head, distance // 2, 1] = dot_nn(probs[distance], grads)
+            if distance == 4:
+                part_copy(head).start()
+        for distance in range(BAND):
+            attended = attended + dot_tn(probs[distance], band[head, distance, 1])
+        for group in range(GROUPS):
             query_head = head * GROUPS + group
             rows = slice(group * TOK, (group + 1) * TOK)
-            columns = head_columns(query_head)
-            att_out[0, :, columns] = attended[rows].astype(BF16)
+            att_buf[query_head] = attended[rows].astype(BF16)
             normed, inverse_q = query_normed(query_head)
-            upstream = dq_scaled[rows] * SCALE
-            query_gain_part = query_gain_part + jnp.sum(upstream * normed, 0, keepdims=True)
-            dq = norm_backward(upstream, normed, inverse_q, q_gain[...])
-            dq_out[0, :, columns] = dq.astype(BF16)
-        both = jnp.concatenate([query_gain_part, key_gain_part], axis=0)
-        gain_part[...] = both if head == 0 else gain_part[...] + both
+            dq = norm_backward(dq_scaled[rows] * SCALE, normed, inverse_q, q_gain[...])
+            dq_buf[query_head] = dq.astype(BF16)
+            store(16 + query_head, att_buf.at[query_head], att_hbm.at[0, :, head_columns(query_head)])
+            store(8 + query_head, dq_buf.at[query_head], dq_hbm.at[0, :, head_columns(query_head)])
+        return later
 
     def send_own(head):
         band_copy(head, NEXT).start()
 
     def pass_on(head):
         band_copy(head, NEXT).wait_recv()
+        if head == 0:
+            band_copy(head, FIRST).wait_recv()
         band_copy(head, RELAY).start()
         band_copy(head, NEAR).start()
 
     def share(head):
         band_copy(head, RELAY).wait_recv()
         band_copy(head, FAR).start()
-
-    def band_ready(head):
-        band_copy(head, NEAR).wait_recv()
-        band_copy(head, FAR).wait_recv()
 
     def join_parts(head):
         part_copy(head).wait_recv()
@@ -315,24 +352,28 @@
         sum_copy(head, 1).wait_recv()
         dk = kept[head, 0, 0] + sum_in[head, 1, 0].astype(F32)
         dv = kept[head, 0, 1] + sum_in[head, 1, 1].astype(F32)
-        dv_out[0, :, head_columns(head)] = dv.astype(BF16)
+        dv_buf[head] = dv.astype(BF16)
         normed, inverse = key_normed(head)
         dk = norm_backward(dk, normed, inverse, k_gain[...])
-        dk_out[0, :, head_columns(head)] = dk.astype(BF16)
-
-    def ar_copies(stage, buffer, mine, size, device_of):
-        sends, arrivals = [], []
-        for step in range(1, size):
-            other = wrap(mine + step, size)
-            device = device_of(other)
-            send = ar_send.at[stage, step]
-            sends.append(remote(buffer.at[mine], buffer.at[mine], send, ar_recv.at[stage, mine], device))
-            arrivals.append(remote(buffer.at[other], buffer.at[other], send, ar_recv.at[stage, other], device))
-        return sends, arrivals
+        dk_buf[head] = dk.astype(BF16)
+        store(4 + head, dv_buf.at[head], dv_hbm.at[0, :, head_columns(head)])
+        store(head, dk_buf.at[head], dk_hbm.at[0, :, head_columns(head)])
 
     def ar_start(stage, buffer, mine, size, device_of, value):
         buffer[mine] = value
-        sends, arrivals = ar_copies(stage, buffer, mine, size, device_of)
+        sends, arrivals = [], []
+        steps = sorted(range(1, size), key=lambda step: -min(step, size - step))
+        for step in steps:
+            other = wrap(mine + step, size)
+            send = ar_send.at[stage, step]
+            sends.append(
+                remote(buffer.at[mine], buffer.at[mine], send, ar_recv.at[stage, mine], device_of(other))
+            )
+            arrivals.append(
+                remote(
+                    buffer.at[other], buffer.at[other], send, ar_recv.at[stage, other], device_of(other)
+                )
+            )
         for copy in sends:
             copy.start()
 
@@ -348,77 +389,70 @@
 
         return finish
 
-    quad = lax.div(z, SIDE)
-    in_quad = lax.rem(z, SIDE)
-
+    pl.semaphore_wait(barrier, len(nearby) + 1)
+    band_copy(0, FIRST).start()
+    loads["k_gain"].wait()
     prepare_keys(0)
-    pl.semaphore_wait(barrier, len(nearby) + 1)
     send_own(0)
     tell(0, nearby)
     prepare_keys(1)
     send_own(1)
     prepare_keys(2)
     prepare_keys(3)
+    loads["q_gain"].wait()
     prepare_queries(0)
     hear(0, len(nearby))
-    tell(1, [along_z(2), along_z(-2)])
+    tell(1, [along_z(2), along_z(-2), along_x(2), along_y(2)])
     prepare_mask()
     pass_on(0)
     send_own(2)
     prepare_queries(1)
-    hear(1, 2)
+    hear(1, 4)
     tell(2, [along_z(4), along_z(-4)])
     pass_on(1)
     send_own(3)
     prepare_queries(2)
     prepare_queries(3)
+    state = begin(0)
     share(0)
-    band_ready(0)
-    attend(0)
+    attend(0, state)
+    pass_on(2)
     hear(2, 2)
     tell(3, [along_z(8), along_z(-8)])
-    pass_on(2)
     join_parts(0)
+    state = begin(1)
     share(1)
-    band_ready(1)
-    attend(1)
-    hear(3, 2)
+    attend(1, state)
     pass_on(3)
     join_parts(1)
     pass_back(0)
+    state = begin(2)
     share(2)
-    band_ready(2)
-    attend(2)
+    attend(2, state)
+    hear(3, 2)
+    share(3)
     join_parts(2)
     pass_back(1)
+    state = begin(3)
+    finish = attend(
+        3,
+        state,
+        lambda: ar_start(0, ar_plane, dp, SIDE * SIDE, lambda other: (other, me), gain_part[...]),
+    )
     finish_keys(0)
-    share(3)
-    band_ready(3)
-    attend(3)
-
-    finish = ar_start(0, ar_x, x, SIDE, lambda other: (y * SIDE + other, me), gain_part[...])
     join_parts(3)
+    finish = ar_start(1, ar_z, z, chips, lambda other: (dp, other * 2 + core), finish())
     pass_back(2)
-    finish = ar_start(1, ar_y, y, SIDE, lambda other: (other * SIDE + x, me), finish())
     finish_keys(1)
-    finish = ar_start(
-        2, ar_z, in_quad, SIDE, lambda other: (dp, (quad * SIDE + other) * 2 + core), finish()
-    )
     pass_back(3)
-    finish = ar_start(
-        3,
-        ar_far,
-        quad,
-        chips // SIDE,
-        lambda other: (dp, (other * SIDE + in_quad) * 2 + core),
-        finish(),
-    )
     finish_keys(2)
     finish_keys(3)
-    finish = ar_start(4, ar_core, core, 2, lambda other: partner, finish())
+    finish = ar_start(2, ar_core, core, 2, lambda other: partner, finish())
     total = finish() * factor
-    q_gain_out[...] = total[0:1]
-    k_gain_out[...] = total[1:2] / k_gain[...]
+    gain_grads[0] = total[0:1]
+    gain_grads[1] = total[1:2] / k_gain[...]
+    store(24, gain_grads.at[0], q_gain_grad_hbm)
+    store(25, gain_grads.at[1], k_gain_grad_hbm)
 
     for head in range(KV_HEADS):
         for kind in range(4):
@@ -426,30 +460,55 @@
         part_copy(head).wait_send()
         for stage in range(2):
             sum_copy(head, stage).wait_send()
+    band_copy(0, FIRST).wait_send()
+    for copy in stores:
+        copy.wait()
+
+
+def hand_over(count, *refs):
+    sources, targets = refs[:count], refs[count : 2 * count]
+    buffers, semaphores = refs[2 * count : 3 * count], refs[3 * count]
+    loads = [
+        pltpu.make_async_copy(source, buffer, semaphores.at[0, slot])
+        for slot, (source, buffer) in enumerate(zip(sources, buffers))
+    ]
+    stores = [
+        pltpu.make_async_copy(buffer, target, semaphores.at[1, slot])
+        for slot, (buffer, target) in enumerate(zip(buffers, targets))
+    ]
+    for load in loads:
+        load.start()
+    for load, store in zip(loads, stores):
+        load.wait()
+        store.start()
+    for store in stores:
+        store.wait()
 
 
 def shards(segment_ids, queries, keys, values, query_gain, key_gain, out_grad):
     ctx_size = lax.axis_size("ctx")
     factor = (lax.axis_size("dp") * queries.shape[0] * ctx_size * queries.shape[1]) ** (-0.5)
     width = KV_HEADS * HEAD_DIM
-    hbm = pl.BlockSpec(memory_space=pltpu.HBM)
-    vmem = pl.BlockSpec(memory_space=pltpu.VMEM)
+    hbm = pl.BlockSpec(memory_space=pl.ANY)
     dma = pltpu.SemaphoreType.DMA
     pair = (2, TOK, HEAD_DIM)
-    quads = ctx_size // 2 // SIDE
+    chips = ctx_size // 2
+    shapes = (
+        jax.ShapeDtypeStruct((1, TOK, HEADS * HEAD_DIM), BF16),
+        jax.ShapeDtypeStruct((1, TOK, HEADS * HEAD_DIM), BF16),
+        jax.ShapeDtypeStruct((1, TOK, width), BF16),
+        jax.ShapeDtypeStruct((1, TOK, width), BF16),
+        jax.ShapeDtypeStruct((1, HEAD_DIM), F32),
+        jax.ShapeDtypeStruct((1, HEAD_DIM), F32),
+    )
     outs = pl.pallas_call(
         lambda *refs: kernel(ctx_size, factor, *refs),
-        out_shape=(
-            jax.ShapeDtypeStruct((1, TOK, HEADS * HEAD_DIM), BF16),
-            jax.ShapeDtypeStruct((1, TOK, HEADS * HEAD_DIM), BF16),
-            jax.ShapeDtypeStruct((1, TOK, width), BF16),
-            jax.ShapeDtypeStruct((1, TOK, width), BF16),
-            jax.ShapeDtypeStruct((1, HEAD_DIM), F32),
-            jax.ShapeDtypeStruct((1, HEAD_DIM), F32),
-        ),
-        in_specs=[hbm, hbm, hbm, hbm, vmem, vmem, hbm],
-        out_specs=(vmem,) * 6,
+        out_shape=shapes,
+        in_specs=[hbm] * 7,
+        out_specs=(hbm,) * len(shapes),
         scratch_shapes=[
+            pltpu.VMEM((1, HEAD_DIM), F32),
+            pltpu.VMEM((1, HEAD_DIM), F32),
             pltpu.VMEM((BAND, 1, TOK), jnp.int32),
             pltpu.VMEM((BAND, TOK, ROWS), F32),
             pltpu.VMEM((HEADS, TOK, HEAD_DIM), BF16),
@@ -462,21 +521,25 @@
             pltpu.VMEM((KV_HEADS, 3) + pair, F32),
             pltpu.VMEM((KV_HEADS, 2) + pair, BF16),
             pltpu.VMEM((KV_HEADS, 2) + pair, BF16),
+            pltpu.VMEM((HEADS, TOK, HEAD_DIM), BF16),
+            pltpu.VMEM((HEADS, TOK, HEAD_DIM), BF16),
+            pltpu.VMEM((KV_HEADS, TOK, HEAD_DIM), BF16),
+            pltpu.VMEM((KV_HEADS, TOK, HEAD_DIM), BF16),
             pltpu.VMEM((2, HEAD_DIM), F32),
-            pltpu.VMEM((SIDE, 2, HEAD_DIM), F32),
-            pltpu.VMEM((SIDE, 2, HEAD_DIM), F32),
-            pltpu.VMEM((SIDE, 2, HEAD_DIM), F32),
-            pltpu.VMEM((quads, 2, HEAD_DIM), F32),
+            pltpu.VMEM((2, 1, HEAD_DIM), F32),
+            pltpu.VMEM((SIDE * SIDE, 2, HEAD_DIM), F32),
+            pltpu.VMEM((chips, 2, HEAD_DIM), F32),
             pltpu.VMEM((2, 2, HEAD_DIM), F32),
-            dma((24 + BAND,)),
-            dma((KV_HEADS, 4)),
-            dma((KV_HEADS, 4)),
+            dma((26 + BAND,)),
+            dma((26,)),
+            dma((KV_HEADS, 5)),
+            dma((KV_HEADS, 5)),
             dma((KV_HEADS,)),
             dma((KV_HEADS,)),
             dma((KV_HEADS, 2)),
             dma((KV_HEADS, 2)),
-            dma((5, quads)),
-            dma((5, quads)),
+            dma((3, chips)),
+            dma((3, chips)),
             pltpu.SemaphoreType.REGULAR((4,)),
         ],
         compiler_params=pltpu.CompilerParams(
@@ -491,6 +554,15 @@
         key_gain.reshape(1, HEAD_DIM),
         out_grad,
     )
+    outs = pl.pallas_call(
+        lambda *refs: hand_over(len(shapes), *refs),
+        out_shape=shapes,
+        in_specs=[hbm] * len(shapes),
+        out_specs=(hbm,) * len(shapes),
+        scratch_shapes=[pltpu.VMEM(shape.shape, shape.dtype) for shape in shapes]
+        + [dma((2, len(shapes)))],
+        compiler_params=pltpu.CompilerParams(vmem_limit_bytes=67043328),
+    )(*outs)
     return (*outs[:4], outs[4].reshape(HEAD_DIM), outs[5].reshape(HEAD_DIM))
 
 

time: 87.2 us -> 76.1 us (0.87)
  local copies, waits for them, and re-layouts: 6.01 us -> 0 us
  Pallas kernels: 80.2 us -> 74.6 us
    unnamed x16 -> x0, local copies, waits for them, and re-layouts: 6.01 us -> none
    pallas_call x1 -> x2, Pallas kernels: 80.2 us -> 74.6 us  [the longest x1 72.3 us: shards(): pl.pallas_call(lambda *refs: kernel(ctx_size, factor, *refs), out_shape=s...]
where the time goes in v2:
time: 76.1 us; the launch traced here: 75.2 us
  Pallas kernels  74.6 us (98%)
    pallas_call x1, Pallas kernels, shards(): pl.pallas_call(lambda *refs: kernel(ctx_size, factor, *refs), out_shape=s...  72.3 us
    pallas_call x1, Pallas kernels, shards(): pl.pallas_call(lambda *refs: hand_over(len(shapes), *refs), out_shape=sha...  2.29 us

profile of v2, /device:TPU:1, one launch (start us, length us, event | category | flops | bytes accessed | tf_op | source)
XLA Modules:
  0.0 75.2 jit_solution(8501014759247847812)
XLA Ops:
  0.6 72.3 %shard_map.118 = (bf16[1,128,2048]{2,1,0:T(8,128)(2,1)}, bf16[1,128,2048]{2,1,0:T(8,128)(2,1)}, bf16[1,128,1024]{2,1,0:T(8,128)(2,1)}, bf16[1,128,1024]{2,1,0:T(...) custom-call(s32[1,8192]{1,0:T(1,128)} %refs_0_.1, bf16[1,128,2048]{2,1,0:T(8,128)(2,1)} %refs_1_.1, ...), custom_call_target="tpu_custom_call" | custom-call | tf_op jit(solution)/shard_map/pallas_call | solution.py:504
  72.9 2.3 %shard_map.119 = (bf16[1,128,2048]{2,1,0:T(8,128)(2,1)}, bf16[1,128,2048]{2,1,0:T(8,128)(2,1)}, bf16[1,128,1024]{2,1,0:T(8,128)(2,1)}, bf16[1,128,1024]{2,1,0:T(...) custom-call(bf16[1,128,2048]{2,1,0:T(8,128)(2,1)} %get-tuple-element.18.refs_0_, ...), custom_call_target="tpu_custom_call" | custom-call | tf_op jit(solution)/shard_map/pallas_call | solution.py:557

commit v3 on v2

--- a/solution.py
+++ b/solution.py
@@ -75,7 +75,7 @@
     mask,
     q_raw,
     q_scaled,
-    out_grad,
+    g_raw,
     k_raw,
     band,
     part_out,
@@ -88,6 +88,7 @@
     dk_buf,
     dv_buf,
     gain_part,
+    gain_rows,
     gain_grads,
     ar_plane,
     ar_z,
@@ -138,23 +139,19 @@
         copy.start()
         loads[name] = copy
 
-    load("k_gain", 24 + BAND, k_gain_hbm, k_gain)
-    load("q_gain", 25 + BAND, q_gain_hbm, q_gain)
-    for head in range(KV_HEADS):
-        load(("k", head), head, k_hbm.at[0, :, head_columns(head)], k_raw.at[head])
-        load(("v", head), 4 + head, v_hbm.at[0, :, head_columns(head)], band.at[head, 0, 1])
+    rest = pl.ds(HEAD_DIM, (KV_HEADS - 1) * HEAD_DIM)
+    load("k_gain", 0, k_gain_hbm, k_gain)
+    load(("k", 0), 1, k_hbm.at[0, :, head_columns(0)], k_raw.at[:, head_columns(0)])
+    load(("v", 0), 2, v_hbm.at[0, :, head_columns(0)], band.at[0, 0, 1])
+    load(("k", 1), 3, k_hbm.at[0, :, rest], k_raw.at[:, rest])
+    for head in range(1, KV_HEADS):
+        load(("v", head), 3 + head, v_hbm.at[0, :, head_columns(head)], band.at[head, 0, 1])
+    load("q_gain", 7, q_gain_hbm, q_gain)
+    load("q", 8, q_hbm.at[0], q_raw)
+    load("g", 9, g_hbm.at[0], g_raw)
     for distance in range(BAND):
         first = pl.multiple_of(jnp.maximum(me - distance, 0) * TOK, TOK)
-        load(("s", distance), 24 + distance, seg_hbm.at[:, pl.ds(first, TOK)], seg_rows.at[distance])
-    for head in range(HEADS):
-        rows = pl.ds((head % GROUPS) * TOK, TOK)
-        load(("q", head), 8 + head, q_hbm.at[0, :, head_columns(head)], q_raw.at[head])
-        load(
-            ("g", head),
-            16 + head,
-            g_hbm.at[0, :, head_columns(head)],
-            out_grad.at[head // GROUPS, rows],
-        )
+        load(("s", distance), 10 + distance, seg_hbm.at[:, pl.ds(first, TOK)], seg_rows.at[distance])
 
     def remote(source, target, send, recv, device):
         return pltpu.make_async_remote_copy(
@@ -182,21 +179,21 @@
         return remote(
             source,
             target,
-            band_send.at[head, kind],
+            band_send,
             band_recv.at[head, kind],
             device,
         )
 
     def part_copy(head):
         return remote(
-            part_out.at[head], part_in.at[head], part_send.at[head], part_recv.at[head], partner
+            part_out.at[head], part_in.at[head], part_send, part_recv.at[head], partner
         )
 
     def sum_copy(head, stage):
         return remote(
             sum_out.at[head, stage],
             sum_in.at[head, stage],
-            sum_send.at[head, stage],
+            sum_send,
             sum_recv.at[head, stage],
             behind,
         )
@@ -209,28 +206,30 @@
         pl.semaphore_wait(known.at[stage], count)
 
     def key_normed(head):
-        field = k_raw[head].astype(F32)
+        field = k_raw[:, head_columns(head)].astype(F32)
         inverse = inverse_norm(field)
         return field * inverse, inverse
 
     def query_normed(head):
-        field = q_raw[head].astype(F32)
+        field = q_raw[:, head_columns(head)].astype(F32)
         inverse = inverse_norm(field)
         return field * inverse, inverse
 
     def prepare_keys(head):
-        loads["k", head].wait()
+        if head < 2:
+            loads["k", head].wait()
         normed, _ = key_normed(head)
         band[head, 0, 0] = (normed * k_gain[...]).astype(BF16)
         loads["v", head].wait()
 
     def prepare_queries(kv_head):
         for group in range(GROUPS):
-            head = kv_head * GROUPS + group
-            loads["q", head].wait()
-            normed, _ = query_normed(head)
+            normed, _ = query_normed(kv_head * GROUPS + group)
             q_scaled[kv_head, pl.ds(group * TOK, TOK)] = (normed * q_gain[...] * SCALE).astype(BF16)
-            loads["g", head].wait()
+
+    def grads_of(kv_head):
+        heads = range(kv_head * GROUPS, (kv_head + 1) * GROUPS)
+        return jnp.concatenate([g_raw[:, head_columns(head)] for head in heads], axis=0)
 
     def prepare_mask():
         for distance in range(BAND):
@@ -260,7 +259,7 @@
     def score(head, distances, state):
         total, weighted, weights, dprobs = state
         queries = q_scaled[head]
-        grads = out_grad[head]
+        grads = grads_of(head)
         for distance in distances:
             weight = jnp.exp(dot_nt(band[head, distance, 0], queries)) * mask[distance]
             dprob = dot_nt(band[head, distance, 1], grads)
@@ -276,10 +275,11 @@
         return score(head, (0, 2, 1), (zero, zero, {}, {}))
 
     def attend(head, state, after_gains=None):
+        state = score(head, (4,), state)
         band_copy(head, FAR).wait_recv()
-        total, weighted, weights, dprobs = score(head, (4, 3), state)
+        total, weighted, weights, dprobs = score(head, (3,), state)
         queries = q_scaled[head]
-        grads = out_grad[head]
+        grads = grads_of(head)
         inverse = 1.0 / total
         centre = weighted * inverse
         probs, dscores = {}, {}
@@ -314,12 +314,11 @@
         for group in range(GROUPS):
             query_head = head * GROUPS + group
             rows = slice(group * TOK, (group + 1) * TOK)
-            att_buf[query_head] = attended[rows].astype(BF16)
+            columns = head_columns(query_head)
+            att_buf[:, columns] = attended[rows].astype(BF16)
             normed, inverse_q = query_normed(query_head)
             dq = norm_backward(dq_scaled[rows] * SCALE, normed, inverse_q, q_gain[...])
-            dq_buf[query_head] = dq.astype(BF16)
-            store(16 + query_head, att_buf.at[query_head], att_hbm.at[0, :, head_columns(query_head)])
-            store(8 + query_head, dq_buf.at[query_head], dq_hbm.at[0, :, head_columns(query_head)])
+            dq_buf[:, columns] = dq.astype(BF16)
         return later
 
     def send_own(head):
@@ -352,42 +351,48 @@
         sum_copy(head, 1).wait_recv()
         dk = kept[head, 0, 0] + sum_in[head, 1, 0].astype(F32)
         dv = kept[head, 0, 1] + sum_in[head, 1, 1].astype(F32)
-        dv_buf[head] = dv.astype(BF16)
+        columns = head_columns(head)
+        dv_buf[:, columns] = dv.astype(BF16)
         normed, inverse = key_normed(head)
         dk = norm_backward(dk, normed, inverse, k_gain[...])
-        dk_buf[head] = dk.astype(BF16)
-        store(4 + head, dv_buf.at[head], dv_hbm.at[0, :, head_columns(head)])
-        store(head, dk_buf.at[head], dk_hbm.at[0, :, head_columns(head)])
-
-    def ar_start(stage, buffer, mine, size, device_of, value):
-        buffer[mine] = value
-        sends, arrivals = [], []
-        steps = sorted(range(1, size), key=lambda step: -min(step, size - step))
-        for step in steps:
-            other = wrap(mine + step, size)
-            send = ar_send.at[stage, step]
-            sends.append(
-                remote(buffer.at[mine], buffer.at[mine], send, ar_recv.at[stage, mine], device_of(other))
-            )
-            arrivals.append(
-                remote(
-                    buffer.at[other], buffer.at[other], send, ar_recv.at[stage, other], device_of(other)
-                )
-            )
-        for copy in sends:
-            copy.start()
-
-        def finish():
-            for copy in arrivals:
-                copy.wait_recv()
-            for copy in sends:
-                copy.wait_send()
-            total = buffer[0]
-            for slot in range(1, size):
-                total = total + buffer[slot]
-            return total
-
-        return finish
+        dk_buf[:, columns] = dk.astype(BF16)
+
+    def ar_copy(stage, source, target, device):
+        return remote(source, target, ar_send.at[stage], ar_recv.at[stage], device)
+
+    def ar_finish(stage, buffer, count):
+        arrived = buffer.at[pl.ds(0, count)]
+        copy = ar_copy(stage, arrived, arrived, partner)
+        copy.wait_recv()
+        copy.wait_send()
+
+    def distance_of(step, size):
+        return min(step, size - step)
+
+    def sum_plane_start():
+        gain_rows[0] = gain_part[0:1]
+        gain_rows[1] = gain_part[1:2]
+        slot = core * SIDE * SIDE + dp
+        ar_plane[slot] = jnp.where(core == 0, gain_part[0:1], gain_part[1:2])
+        steps = [(dy, dx) for dy in range(SIDE) for dx in range(SIDE)]
+        for dy, dx in sorted(steps, key=lambda step: -sum(distance_of(each, SIDE) for each in step)):
+            other = wrap(y + dy, SIDE) * SIDE + wrap(x + dx, SIDE)
+            ar_copy(0, gain_rows.at[1 - core], ar_plane.at[slot], (other, partner[1])).start()
+            if (dy, dx) != (0, 0):
+                ar_copy(0, gain_rows.at[core], ar_plane.at[slot], (other, me)).start()
+
+    def sum_z_start():
+        ar_finish(0, ar_plane, 2 * SIDE * SIDE - 1)
+        ar_z[z] = jnp.sum(ar_plane[...], 0)
+        for step in sorted(range(1, chips), key=lambda step: -distance_of(step, chips)):
+            other = wrap(z + step, chips)
+            ar_copy(1, ar_z.at[z], ar_z.at[z], (dp, other * 2 + core)).start()
+
+    def share_rows():
+        ar_finish(1, ar_z, chips - 1)
+        ar_core[core] = jnp.sum(ar_z[...], 0)
+        ar_copy(2, ar_core.at[core], ar_core.at[core], partner).start()
+        ar_finish(2, ar_core, 1)
 
     pl.semaphore_wait(barrier, len(nearby) + 1)
     band_copy(0, FIRST).start()
@@ -400,6 +405,7 @@
     prepare_keys(2)
     prepare_keys(3)
     loads["q_gain"].wait()
+    loads["q"].wait()
     prepare_queries(0)
     hear(0, len(nearby))
     tell(1, [along_z(2), along_z(-2), along_x(2), along_y(2)])
@@ -408,16 +414,17 @@
     send_own(2)
     prepare_queries(1)
     hear(1, 4)
-    tell(2, [along_z(4), along_z(-4)])
+    tell(2, [along_z(4), along_z(-4), partner])
     pass_on(1)
     send_own(3)
     prepare_queries(2)
     prepare_queries(3)
+    loads["g"].wait()
     state = begin(0)
     share(0)
     attend(0, state)
     pass_on(2)
-    hear(2, 2)
+    hear(2, 3)
     tell(3, [along_z(8), along_z(-8)])
     join_parts(0)
     state = begin(1)
@@ -430,37 +437,37 @@
     share(2)
     attend(2, state)
     hear(3, 2)
+    state = begin(3)
     share(3)
+    attend(3, state, sum_plane_start)
+    store(0, att_buf, att_hbm.at[0])
+    store(1, dq_buf, dq_hbm.at[0])
     join_parts(2)
     pass_back(1)
-    state = begin(3)
-    finish = attend(
-        3,
-        state,
-        lambda: ar_start(0, ar_plane, dp, SIDE * SIDE, lambda other: (other, me), gain_part[...]),
-    )
     finish_keys(0)
     join_parts(3)
-    finish = ar_start(1, ar_z, z, chips, lambda other: (dp, other * 2 + core), finish())
+    sum_z_start()
     pass_back(2)
     finish_keys(1)
     pass_back(3)
     finish_keys(2)
+    early = pl.ds(0, (KV_HEADS - 1) * HEAD_DIM)
+    last = head_columns(KV_HEADS - 1)
+    store(2, dk_buf.at[:, early], dk_hbm.at[0, :, early])
+    store(3, dv_buf.at[:, early], dv_hbm.at[0, :, early])
     finish_keys(3)
-    finish = ar_start(2, ar_core, core, 2, lambda other: partner, finish())
-    total = finish() * factor
-    gain_grads[0] = total[0:1]
-    gain_grads[1] = total[1:2] / k_gain[...]
-    store(24, gain_grads.at[0], q_gain_grad_hbm)
-    store(25, gain_grads.at[1], k_gain_grad_hbm)
-
-    for head in range(KV_HEADS):
-        for kind in range(4):
-            band_copy(head, kind).wait_send()
-        part_copy(head).wait_send()
-        for stage in range(2):
-            sum_copy(head, stage).wait_send()
-    band_copy(0, FIRST).wait_send()
+    store(4, dk_buf.at[:, last], dk_hbm.at[0, :, last])
+    store(5, dv_buf.at[:, last], dv_hbm.at[0, :, last])
+    share_rows()
+    gain_grads[0] = ar_core[0] * factor
+    gain_grads[1] = ar_core[1] * factor / k_gain[...]
+    store(6, gain_grads.at[0], q_gain_grad_hbm)
+    store(7, gain_grads.at[1], k_gain_grad_hbm)
+
+    sent = band.at[:, pl.ds(0, 4)]
+    remote(sent, sent, band_send, band_recv.at[0, 0], ahead).wait_send()
+    remote(part_out, part_out, part_send, part_recv.at[0], partner).wait_send()
+    remote(sum_out, sum_out, sum_send, sum_recv.at[0, 0], behind).wait_send()
     for copy in stores:
         copy.wait()
 
@@ -511,35 +518,36 @@
             pltpu.VMEM((1, HEAD_DIM), F32),
             pltpu.VMEM((BAND, 1, TOK), jnp.int32),
             pltpu.VMEM((BAND, TOK, ROWS), F32),
-            pltpu.VMEM((HEADS, TOK, HEAD_DIM), BF16),
+            pltpu.VMEM((TOK, HEADS * HEAD_DIM), BF16),
             pltpu.VMEM((KV_HEADS, ROWS, HEAD_DIM), BF16),
-            pltpu.VMEM((KV_HEADS, ROWS, HEAD_DIM), BF16),
-            pltpu.VMEM((KV_HEADS, TOK, HEAD_DIM), BF16),
+            pltpu.VMEM((TOK, HEADS * HEAD_DIM), BF16),
+            pltpu.VMEM((TOK, width), BF16),
             pltpu.VMEM((KV_HEADS, BAND) + pair, BF16),
             pltpu.VMEM((KV_HEADS, 2) + pair, BF16),
             pltpu.VMEM((KV_HEADS, 2) + pair, BF16),
             pltpu.VMEM((KV_HEADS, 3) + pair, F32),
             pltpu.VMEM((KV_HEADS, 2) + pair, BF16),
             pltpu.VMEM((KV_HEADS, 2) + pair, BF16),
-            pltpu.VMEM((HEADS, TOK, HEAD_DIM), BF16),
-            pltpu.VMEM((HEADS, TOK, HEAD_DIM), BF16),
-            pltpu.VMEM((KV_HEADS, TOK, HEAD_DIM), BF16),
-            pltpu.VMEM((KV_HEADS, TOK, HEAD_DIM), BF16),
+            pltpu.VMEM((TOK, HEADS * HEAD_DIM), BF16),
+            pltpu.VMEM((TOK, HEADS * HEAD_DIM), BF16),
+            pltpu.VMEM((TOK, width), BF16),
+            pltpu.VMEM((TOK, width), BF16),
             pltpu.VMEM((2, HEAD_DIM), F32),
             pltpu.VMEM((2, 1, HEAD_DIM), F32),
-            pltpu.VMEM((SIDE * SIDE, 2, HEAD_DIM), F32),
-            pltpu.VMEM((chips, 2, HEAD_DIM), F32),
-            pltpu.VMEM((2, 2, HEAD_DIM), F32),
-            dma((26 + BAND,)),
-            dma((26,)),
+            pltpu.VMEM((2, 1, HEAD_DIM), F32),
+            pltpu.VMEM((2 * SIDE * SIDE, 1, HEAD_DIM), F32),
+            pltpu.VMEM((chips, 1, HEAD_DIM), F32),
+            pltpu.VMEM((2, 1, HEAD_DIM), F32),
+            dma((10 + BAND,)),
+            dma((8,)),
+            dma,
             dma((KV_HEADS, 5)),
-            dma((KV_HEADS, 5)),
+            dma,
             dma((KV_HEADS,)),
-            dma((KV_HEADS,)),
+            dma,
             dma((KV_HEADS, 2)),
-            dma((KV_HEADS, 2)),
-            dma((3, chips)),
-            dma((3, chips)),
+            dma((3,)),
+            dma((3,)),
             pltpu.SemaphoreType.REGULAR((4,)),
         ],
         compiler_params=pltpu.CompilerParams(

time: 76.1 us -> 74.2 us (0.975)
  the two profiles are of different devices: /device:TPU:1 before, /device:TPU:63 now
where the time goes in v3:
time: 74.2 us; the launch traced here: 74 us
  Pallas kernels  73.3 us (99%)
    pallas_call x1, Pallas kernels, shards(): pl.pallas_call(lambda *refs: kernel(ctx_size, factor, *refs), out_shape=s...  71.1 us
    pallas_call x1, Pallas kernels, shards(): pl.pallas_call(lambda *refs: hand_over(len(shapes), *refs), out_shape=sha...  2.29 us

profile of v3, /device:TPU:63, one launch (start us, length us, event | category | flops | bytes accessed | tf_op | source)
XLA Modules:
  0.0 74.0 jit_solution(3139590898808121793)
XLA Ops:
  0.6 71.1 %shard_map.118 = (bf16[1,128,2048]{2,1,0:T(8,128)(2,1)}, bf16[1,128,2048]{2,1,0:T(8,128)(2,1)}, bf16[1,128,1024]{2,1,0:T(8,128)(2,1)}, bf16[1,128,1024]{2,1,0:T(...) custom-call(s32[1,8192]{1,0:T(1,128)} %refs_0_.1, bf16[1,128,2048]{2,1,0:T(8,128)(2,1)} %refs_1_.1, ...), custom_call_target="tpu_custom_call" | custom-call | tf_op jit(solution)/shard_map/pallas_call | solution.py:511
  71.7 2.3 %shard_map.119 = (bf16[1,128,2048]{2,1,0:T(8,128)(2,1)}, bf16[1,128,2048]{2,1,0:T(8,128)(2,1)}, bf16[1,128,1024]{2,1,0:T(8,128)(2,1)}, bf16[1,128,1024]{2,1,0:T(...) custom-call(bf16[1,128,2048]{2,1,0:T(8,128)(2,1)} %get-tuple-element.18.refs_0_, ...), custom_call_target="tpu_custom_call" | custom-call | tf_op jit(solution)/shard_map/pallas_call | solution.py:565

commit v4 on v3

--- a/solution.py
+++ b/solution.py
@@ -331,9 +331,16 @@
         band_copy(head, RELAY).start()
         band_copy(head, NEAR).start()
 
+        @pl.when(core == 0)
+        def _():
+            band_copy(head, FAR).start()
+
     def share(head):
         band_copy(head, RELAY).wait_recv()
-        band_copy(head, FAR).start()
+
+        @pl.when(core == 1)
+        def _():
+            band_copy(head, FAR).start()
 
     def join_parts(head):
         part_copy(head).wait_recv()
@@ -439,11 +446,11 @@
     hear(3, 2)
     state = begin(3)
     share(3)
+    join_parts(2)
+    pass_back(1)
     attend(3, state, sum_plane_start)
     store(0, att_buf, att_hbm.at[0])
     store(1, dq_buf, dq_hbm.at[0])
-    join_parts(2)
-    pass_back(1)
     finish_keys(0)
     join_parts(3)
     sum_z_start()

time: 74.2 us -> 71.1 us (0.958)
  the two profiles are of different devices: /device:TPU:63 before, /device:TPU:1 now
where the time goes in v4:
time: 71.1 us; the launch traced here: 70.9 us
  Pallas kernels  70.2 us (99%)
    pallas_call x1, Pallas kernels, shards(): pl.pallas_call(lambda *refs: kernel(ctx_size, factor, *refs), out_shape=s...  68 us
    pallas_call x1, Pallas kernels, shards(): pl.pallas_call(lambda *refs: hand_over(len(shapes), *refs), out_shape=sha...  2.29 us

profile of v4, /device:TPU:1, one launch (start us, length us, event | category | flops | bytes accessed | tf_op | source)
XLA Modules:
  0.0 70.9 jit_solution(15867954223740370409)
XLA Ops:
  0.6 68.0 %shard_map.118 = (bf16[1,128,2048]{2,1,0:T(8,128)(2,1)}, bf16[1,128,2048]{2,1,0:T(8,128)(2,1)}, bf16[1,128,1024]{2,1,0:T(8,128)(2,1)}, bf16[1,128,1024]{2,1,0:T(...) custom-call(s32[1,8192]{1,0:T(1,128)} %refs_0_.1, bf16[1,128,2048]{2,1,0:T(8,128)(2,1)} %refs_1_.1, ...), custom_call_target="tpu_custom_call" | custom-call | tf_op jit(solution)/shard_map/pallas_call | solution.py:518
  68.6 2.3 %shard_map.119 = (bf16[1,128,2048]{2,1,0:T(8,128)(2,1)}, bf16[1,128,2048]{2,1,0:T(8,128)(2,1)}, bf16[1,128,1024]{2,1,0:T(8,128)(2,1)}, bf16[1,128,1024]{2,1,0:T(...) custom-call(bf16[1,128,2048]{2,1,0:T(8,128)(2,1)} %get-tuple-element.18.refs_0_, ...), custom_call_target="tpu_custom_call" | custom-call | tf_op jit(solution)/shard_map/pallas_call | solution.py:572
